TPU v7x, 32 devices: a whole 2x2x4 slice. The times are simulated.
32 devices in a mesh: section: 4 (over x, core), seq: 8 (over z, y).
Axes of the slice: x: 2, y: 2, z: 4, core: 2. Of those that a mesh axis runs over, the one named last changes fastest.
Arguments:
- layer_input: bfloat16 [4, 512, 4, 1536], P('section', 'seq'), may hold values from -300 to 300
- norm_gain: float32 [4, 1536], P('section'), may hold values from 0.1 to 1.9
- queries: bfloat16 [4, 512, 4, 1024], P('section', 'seq'), may hold values from -6 to 6
- key_states: bfloat16 [4, 512, 4, 1024], P('section', 'seq'), may hold values from -6 to 6
- value_states: bfloat16 [4, 512, 4, 1024], P('section', 'seq'), may hold values from -6 to 6
- out_grad: bfloat16 [4, 512, 4, 1536], P('section', 'seq'), may hold values from -6 to 6
- out_weight: bfloat16 [4, 1024, 1536], P('section', 'seq'), may hold values from -0.1875 to 0.1875
- qkv_weight: bfloat16 [4, 1536, 3072], P('section', 'seq'), may hold values from -0.15625 to 0.15625
- lengths: int32 [4, 4], P('section'), may hold values from 256 to 512
Outputs:
- passed_grad: bfloat16 [4, 512, 4, 1536], P('section', 'seq')
All inputs are finite; a program needn't handle non-finite values.
Results may differ from a plain program's by a relative error of at most 0.0034.
Values may be sent and summed in bfloat16 or wider, within the bound.
A program may use at most 128 MiB of HBM per device.

v0:
```python
import jax
import jax.numpy as jnp
from jax import lax
from jax.sharding import PartitionSpec as P

HEADS = 16
HS = 64
EPSILON = 1e-05
MASKED = -1e30
ROW_DOT = (((1,), (1,)), ((), ()))
COL_DOT = (((0,), (0,)), ((), ()))


def shifted(shard, axis, by):
    count = lax.axis_size(axis)
    return lax.ppermute(shard, axis, [(i, (i + by) % count) for i in range(count)])


def item_backward(query_rows, key_rows, value_rows, grad_rows, key_valid):
    length = query_rows.shape[0]
    block = min(512, length)
    scale = HS ** (-0.5)
    offsets = jnp.arange(0, length, block)
    zeros = jnp.zeros((length, query_rows.shape[1]), jnp.float32)

    def step(carry, offset):
        key_total, value_total = carry
        query_block = lax.dynamic_slice_in_dim(query_rows, offset, block, 0)
        grad_block = lax.dynamic_slice_in_dim(grad_rows, offset, block, 0)
        scores = (
            lax.dot_general(query_block, key_rows, ROW_DOT, preferred_element_type=jnp.float32)
            * scale
        )
        scores = jnp.where(key_valid[None, :], scores, MASKED)
        largest = jnp.max(scores, axis=1, keepdims=True)
        weights = jnp.exp(scores - largest)
        probs = weights / jnp.sum(weights, axis=1, keepdims=True)
        probs_low = probs.astype(jnp.bfloat16)
        grad_probs = lax.dot_general(
            grad_block, value_rows, ROW_DOT, preferred_element_type=jnp.float32
        )
        centre = jnp.sum(probs * grad_probs, axis=1, keepdims=True)
        grad_scores = (probs * (grad_probs - centre) * scale).astype(jnp.bfloat16)
        query_grad = jnp.dot(grad_scores, key_rows, preferred_element_type=jnp.float32)
        key_total = key_total + lax.dot_general(
            grad_scores, query_block, COL_DOT, preferred_element_type=jnp.float32
        )
        value_total = value_total + lax.dot_general(
            probs_low, grad_block, COL_DOT, preferred_element_type=jnp.float32
        )
        return ((key_total, value_total), query_grad.astype(jnp.bfloat16))

    (key_total, value_total), query_parts = lax.scan(step, (zeros, zeros), offsets)
    query_grad = query_parts.reshape(length, query_rows.shape[1])
    return (query_grad, key_total.astype(jnp.bfloat16), value_total.astype(jnp.bfloat16))


def split_items(columns):
    length = columns.shape[0]
    count = columns.shape[1] // HS
    return columns.reshape(length, count, HS).transpose(1, 0, 2)


def join_items(items):
    count = items.shape[0]
    length = items.shape[1]
    return items.transpose(1, 0, 2).reshape(length, count * HS)


def project_grad(flat_grad, out_rows):
    return lax.dot_general(
        flat_grad,
        lax.all_gather(out_rows, "seq", axis=0, tiled=True),
        ROW_DOT,
        preferred_element_type=jnp.float32,
    ).astype(jnp.bfloat16)


def on_device(
    layer_input,
    norm_gain,
    queries,
    key_states,
    value_states,
    out_grad,
    out_weight,
    qkv_weight,
    lengths,
):
    frames = queries.shape[1]
    records = queries.shape[2]
    features = queries.shape[3]
    model_width = out_grad.shape[3]
    flat_grad = out_grad[0].reshape(frames * records, model_width)
    frame_queries = queries[0].reshape(frames, records * features)
    frame_keys = key_states[0].reshape(frames, records * features)
    frame_values = value_states[0].reshape(frames, records * features)
    attn_grad = project_grad(flat_grad, out_weight[0])
    head_queries, head_keys, head_values, head_grads = (
        lax.all_to_all(frame_queries, "seq", split_axis=1, concat_axis=0, tiled=True),
        lax.all_to_all(frame_keys, "seq", split_axis=1, concat_axis=0, tiled=True),
        lax.all_to_all(frame_values, "seq", split_axis=1, concat_axis=0, tiled=True),
        lax.all_to_all(
            attn_grad.reshape(frames, records * features),
            "seq",
            split_axis=1,
            concat_axis=0,
            tiled=True,
        ),
    )
    items_here = head_queries.shape[1] // HS
    length = head_queries.shape[0]
    item_ids = lax.axis_index("seq") * items_here + jnp.arange(items_here, dtype=jnp.int32)
    record_ids = item_ids // HEADS
    record_pick = jnp.arange(records, dtype=jnp.int32)[None, :] == record_ids[:, None]
    item_lengths = jnp.sum(jnp.where(record_pick, lengths[0][None, :], 0), axis=1)
    key_valid = jnp.arange(length, dtype=jnp.int32)[None, :] < item_lengths[:, None]
    query_grad, key_gradient, value_grad = lax.map(
        lambda group: item_backward(*group),
        (
            split_items(head_queries),
            split_items(head_keys),
            split_items(head_values),
            split_items(head_grads),
            key_valid,
        ),
    )
    query_back, key_backward, value_back = (
        lax.all_to_all(join_items(query_grad), "seq", split_axis=0, concat_axis=1, tiled=True),
        lax.all_to_all(join_items(key_gradient), "seq", split_axis=0, concat_axis=1, tiled=True),
        lax.all_to_all(join_items(value_grad), "seq", split_axis=0, concat_axis=1, tiled=True),
    )
    joined = jnp.concatenate(
        [
            query_back.reshape(frames * records, features),
            key_backward.reshape(frames * records, features),
            value_back.reshape(frames * records, features),
        ],
        axis=1,
    )
    norm_grad = lax.dot_general(
        joined,
        lax.all_gather(qkv_weight[0], "seq", axis=0, tiled=True),
        ROW_DOT,
        preferred_element_type=jnp.float32,
    )
    inputs = layer_input[0].reshape(frames * records, model_width).astype(jnp.float32)
    row_average = jnp.mean(inputs, axis=1, keepdims=True)
    centered_input = inputs - row_average
    var = jnp.mean(centered_input * centered_input, axis=1, keepdims=True)
    inverse_deviation = 1.0 / jnp.sqrt(var + EPSILON)
    normalized_input = centered_input * inverse_deviation
    scaled_rows = norm_grad * norm_gain[0][None, :]
    residual_branch = inverse_deviation * (
        scaled_rows
        - jnp.mean(scaled_rows, axis=1, keepdims=True)
        - normalized_input * jnp.mean(scaled_rows * normalized_input, axis=1, keepdims=True)
    )
    input_grad = (flat_grad.astype(jnp.float32) + residual_branch).astype(jnp.bfloat16)
    input_grad = input_grad.reshape(1, frames, records, model_width)
    return shifted(input_grad, "section", -1)


def solution(mesh):
    in_specs = (
        P("section", "seq", None, None),
        P("section", None),
        P("section", "seq", None, None),
        P("section", "seq", None, None),
        P("section", "seq", None, None),
        P("section", "seq", None, None),
        P("section", "seq", None),
        P("section", "seq", None),
        P("section", None),
    )
    out_specs = P("section", "seq", None, None)
    return jax.shard_map(
        on_device, mesh=mesh, in_specs=in_specs, out_specs=out_specs, check_vma=False
    )
```

profile of v0, /device:TPU:1, one launch (start us, length us, event | category | flops | bytes accessed | tf_op | source)
XLA Modules:
  0.0 301.7 jit_solution(11840325789857754773)
XLA Ops:
  9.4 6.4 %all-to-all-start = ((bf16[64,8,512]{2,0,1:T(8,128)(2,1)}), bf16[64,8,512]{2,0,1:T(8,128)(2,1)S(1)}, u32[]{:S(2)}, u32[]{:S(2)}) async-start(bf16[64,8,512]{2,0,1:T(8,128)(2,1)} %copy.24), calls=%async_computation | async-start | bytes 1048576 | tf_op jit(solution)/shard_map/all_to_all | solution.py:100
  16.9 14.0 %all-to-all-done = bf16[64,8,512]{2,0,1:T(8,128)(2,1)S(1)} async-done(((bf16[64,8,512]{2,0,1:T(8,128)(2,1)}), bf16[64,8,512]{2,0,1:T(8,128)(2,1)S(1)}, u32[]{:S(2)}, u32[]{:S(2)}) %all-to-all-start) | async-done | bytes 524320 | tf_op jit(solution)/shard_map/all_to_all | solution.py:100
  31.0 13.1 %all-to-all-start.1 = ((bf16[64,8,512]{2,0,1:T(8,128)(2,1)}), bf16[64,8,512]{2,0,1:T(8,128)(2,1)S(1)}, u32[]{:S(2)}, u32[]{:S(2)}) async-start(bf16[64,8,512]{2,0,1:T(8,128)(2,1)} %copy.25), calls=%async_computation.1 | async-start | bytes 1048576 | tf_op jit(solution)/shard_map/all_to_all | solution.py:101
  45.1 15.1 %all-to-all-done.1 = bf16[64,8,512]{2,0,1:T(8,128)(2,1)S(1)} async-done(((bf16[64,8,512]{2,0,1:T(8,128)(2,1)}), bf16[64,8,512]{2,0,1:T(8,128)(2,1)S(1)}, u32[]{:S(2)}, u32[]{:S(2)}) %all-to-all-start.1) | async-done | bytes 524320 | tf_op jit(solution)/shard_map/all_to_all | solution.py:101
  60.3 14.4 %all-to-all-start.3 = ((bf16[64,8,512]{2,0,1:T(8,128)(2,1)}), bf16[64,8,512]{2,0,1:T(8,128)(2,1)S(1)}, u32[]{:S(2)}, u32[]{:S(2)}) async-start(bf16[64,8,512]{2,0,1:T(8,128)(2,1)} %copy.27), calls=%async_computation.3 | async-start | bytes 1048576 | tf_op jit(solution)/shard_map/all_to_all | solution.py:102
  74.9 18.9 %all-gather.5.cloned.1.call-done = bf16[1,1024,1536]{2,1,0:T(8,128)(2,1)} async-done(((bf16[1,128,1536]{2,1,0:T(8,128)(2,1)}), bf16[1,1024,1536]{2,1,0:T(8,128)(2,1)}) %all-gather.5.cloned.1.call-update) | async-done | bytes 3145744 | tf_op jit(solution)/shard_map/all_gather | solution.py:73
  93.8 2.9 fusion.43
  97.9 4.1 %all-to-all-start.2 = ((bf16[64,8,512]{2,0,1:T(8,128)(2,1)}), bf16[64,8,512]{2,0,1:T(8,128)(2,1)}, u32[]{:S(2)}, u32[]{:S(2)}) async-start(bf16[64,8,512]{2,0,1:T(8,128)(2,1)} %copy.26), calls=%async_computation.2 | async-start | bytes 1048576 | tf_op jit(solution)/shard_map/all_to_all | solution.py:103
  103.7 1.6 reshape.134
  105.5 1.6 reshape.136
  108.3 7.5 %all-to-all-done.2 = bf16[64,8,512]{2,0,1:T(8,128)(2,1)} async-done(((bf16[64,8,512]{2,0,1:T(8,128)(2,1)}), bf16[64,8,512]{2,0,1:T(8,128)(2,1)}, u32[]{:S(2)}, u32[]{:S(2)}) %all-to-all-start.2) | async-done | bytes 524320 | tf_op jit(solution)/shard_map/all_to_all | solution.py:103
  115.8 1.6 reshape.135
  118.7 46.5 %while.14 = (s32[]{:T(128)}, bf16[8,512,64]{1,2,0:T(8,128)(2,1)}, bf16[8,512,64]{1,2,0:T(8,128)(2,1)}, bf16[8,512,64]{1,2,0:T(8,128)(2,1)}, pred[8,512]{1,0:T(8,...) while((s32[]{:T(128)}, bf16[8,512,64]{1,2,0:T(8,128)(2,1)}, ...), condition=%wide.region_7.8_spmd, body=%wide.region_3.7_spmd.sunk | while | flops 172587520 | bytes 10056297 | solution.py:118
  119.2 1.8 fusion.73
  125.0 1.8 fusion.73
  130.8 1.9 fusion.73
  136.6 1.9 fusion.73
  142.4 1.9 fusion.73
  148.2 1.8 fusion.73
  154.0 1.8 fusion.73
  159.8 1.8 fusion.73
  165.1 1.6 reshape.144
  166.8 1.5 copy.38
  168.3 4.4 %all-to-all-start.4 = ((bf16[8,64,512]{2,1,0:T(8,128)(2,1)}), bf16[8,64,512]{2,1,0:T(8,128)(2,1)S(1)}, u32[]{:S(2)}, u32[]{:S(2)}) async-start(bf16[8,64,512]{2,1,0:T(8,128)(2,1)} %copy.38), calls=%async_computation.4 | async-start | bytes 1048576 | tf_op jit(solution)/shard_map/all_to_all | solution.py:129
  174.9 25.2 %all-to-all-done.4 = bf16[8,64,512]{2,1,0:T(8,128)(2,1)S(1)} async-done(((bf16[8,64,512]{2,1,0:T(8,128)(2,1)}), bf16[8,64,512]{2,1,0:T(8,128)(2,1)S(1)}, u32[]{:S(2)}, u32[]{:S(2)}) %all-to-all-start.4) | async-done | bytes 524320 | tf_op jit(solution)/shard_map/all_to_all | solution.py:129
  200.1 6.2 %all-to-all-start.5 = ((bf16[8,64,512]{2,1,0:T(8,128)(2,1)}), bf16[8,64,512]{2,1,0:T(8,128)(2,1)S(1)}, u32[]{:S(2)}, u32[]{:S(2)}) async-start(bf16[8,64,512]{2,1,0:T(8,128)(2,1)} %copy.39), calls=%async_computation.5 | async-start | bytes 1048576 | tf_op jit(solution)/shard_map/all_to_all | solution.py:130
  208.4 24.6 %all-to-all-done.5 = bf16[8,64,512]{2,1,0:T(8,128)(2,1)S(1)} async-done(((bf16[8,64,512]{2,1,0:T(8,128)(2,1)}), bf16[8,64,512]{2,1,0:T(8,128)(2,1)S(1)}, u32[]{:S(2)}, u32[]{:S(2)}) %all-to-all-start.5) | async-done | bytes 524320 | tf_op jit(solution)/shard_map/all_to_all | solution.py:130
  232.9 6.7 %all-to-all-start.6 = ((bf16[8,64,512]{2,1,0:T(8,128)(2,1)}), bf16[8,64,512]{2,1,0:T(8,128)(2,1)}, u32[]{:S(2)}, u32[]{:S(2)}) async-start(bf16[8,64,512]{2,1,0:T(8,128)(2,1)} %copy.40), calls=%async_computation.6 | async-start | bytes 1048576 | tf_op jit(solution)/shard_map/all_to_all | solution.py:131
  242.8 23.1 %all-to-all-done.6 = bf16[8,64,512]{2,1,0:T(8,128)(2,1)} async-done(((bf16[8,64,512]{2,1,0:T(8,128)(2,1)}), bf16[8,64,512]{2,1,0:T(8,128)(2,1)}, u32[]{:S(2)}, u32[]{:S(2)}) %all-to-all-start.6) | async-done | bytes 524320 | tf_op jit(solution)/shard_map/all_to_all | solution.py:131
  268.2 6.5 %all-gather.7.cloned.1.call-done = bf16[1,1536,3072]{2,1,0:T(8,128)(2,1)} async-done(((bf16[1,192,3072]{2,1,0:T(8,128)(2,1)}), bf16[1,1536,3072]{2,1,0:T(8,128)(2,1)}) %all-gather.7.cloned.1.call-update) | async-done | bytes 9437200 | tf_op jit(solution)/shard_map/all_gather | solution.py:143
  274.7 6.7 %fusion.47 = (f32[256]{0:T(256)S(1)}, f32[256]{0:T(256)S(1)}, f32[256,1536]{1,0:T(8,128)S(1)}) fusion(f32[256]{0:T(256)S(1)} %sqrt.6, f32[256,1536]{1,0:T(8,128)S(1)} %reshape.141, f32[256]{0:T(256)S(1)} %div.47, f32[1536]{0:T(1024)S(1)} %reduce.3, bf16[1,1536,3072]{2,1,0:T(8,128)(2,1)} %all-gather.7.cloned.1.call-done, bf16[256,1024]{1,0:T(8,128)(2,1)} %reshape.139, ...), kind=kOutput, calls=%fused_computation.66 | convolution fusion | flops 2422996480 | bytes 14166016 | tf_op jit(solution)/shard_map/dot_general | solution.py:141
  283.2 10.7 %collective-permute-done = bf16[1,64,4,1536]{3,2,1,0:T(4,128)(2,1)S(1)} collective-permute-done((bf16[1,64,4,1536]{3,2,1,0:T(4,128)(2,1)S(1)}, bf16[1,64,4,1536]{3,2,1,0:T(4,128)(2,1)S(1)}, u32[]{:S(2)}, u32[]{:S(2)}) %collective-permute-start) | collective-permute-done | bytes 786464 | tf_op jit(solution)/shard_map/ppermute | solution.py:16
  (130 shorter events, 54.1 us)
Async XLA Ops:
  6.5 87.3 %all-gather.5.cloned.1.call-start = ((), (), s32[]{:S(2)}) async-start(), calls=%async_computation.7 | async-start | bytes 3538944 | tf_op jit(solution)/shard_map/all_gather | solution.py:73
  7.3 8.6 %copy-start.8 = (bf16[1,64,4,1024]{3,2,1,0:T(4,128)(2,1)S(1)}, bf16[1,64,4,1024]{3,2,1,0:T(4,128)(2,1)}, u32[]{:S(2)}) copy-start(bf16[1,64,4,1024]{3,2,1,0:T(4,128)(2,1)} %param.14) | copy-start | bytes 1572868
  9.4 21.5 %all-to-all-start = ((bf16[64,8,512]{2,0,1:T(8,128)(2,1)}), bf16[64,8,512]{2,0,1:T(8,128)(2,1)S(1)}, u32[]{:S(2)}, u32[]{:S(2)}) async-start(bf16[64,8,512]{2,0,1:T(8,128)(2,1)} %copy.24), calls=%async_computation | async-start | bytes 1048576 | tf_op jit(solution)/shard_map/all_to_all | solution.py:100
  15.8 28.2 %copy-start.9 = (bf16[1,64,4,1024]{3,2,1,0:T(4,128)(2,1)S(1)}, bf16[1,64,4,1024]{3,2,1,0:T(4,128)(2,1)}, u32[]{:S(2)}) copy-start(bf16[1,64,4,1024]{3,2,1,0:T(4,128)(2,1)} %param.15) | copy-start | bytes 1572868
  31.0 29.3 %all-to-all-start.1 = ((bf16[64,8,512]{2,0,1:T(8,128)(2,1)}), bf16[64,8,512]{2,0,1:T(8,128)(2,1)S(1)}, u32[]{:S(2)}, u32[]{:S(2)}) async-start(bf16[64,8,512]{2,0,1:T(8,128)(2,1)} %copy.25), calls=%async_computation.1 | async-start | bytes 1048576 | tf_op jit(solution)/shard_map/all_to_all | solution.py:101
  44.0 30.7 %copy-start.5 = (bf16[1,64,4,1536]{3,2,1,0:T(4,128)(2,1)S(1)}, bf16[1,64,4,1536]{3,2,1,0:T(4,128)(2,1)}, u32[]{:S(2)}) copy-start(bf16[1,64,4,1536]{3,2,1,0:T(4,128)(2,1)} %param.16) | copy-start | bytes 2359300
  60.3 36.4 %copy-start.3 = (bf16[64,8,512]{2,0,1:T(8,128)(2,1)}, bf16[64,8,512]{2,0,1:T(8,128)(2,1)S(1)}, u32[]{:S(2)}) copy-start(bf16[64,8,512]{2,0,1:T(8,128)(2,1)S(1)} %all-to-all-done.1) | copy-start | bytes 1572868
  60.3 37.6 %all-to-all-start.3 = ((bf16[64,8,512]{2,0,1:T(8,128)(2,1)}), bf16[64,8,512]{2,0,1:T(8,128)(2,1)S(1)}, u32[]{:S(2)}, u32[]{:S(2)}) async-start(bf16[64,8,512]{2,0,1:T(8,128)(2,1)} %copy.27), calls=%async_computation.3 | async-start | bytes 1048576 | tf_op jit(solution)/shard_map/all_to_all | solution.py:102
  74.9 21.8 %copy-start.1 = (bf16[256,1536]{1,0:T(8,128)(2,1)}, bf16[256,1536]{1,0:T(8,128)(2,1)S(1)}, u32[]{:S(2)}) copy-start(bf16[256,1536]{1,0:T(8,128)(2,1)S(1)} %reshape_squeeze.2) | copy-start | bytes 2359300
  96.9 5.9 %copy-start.12 = (s32[1,4]{1,0:T(1,128)S(1)}, s32[1,4]{1,0:T(1,128)}, u32[]{:S(2)}) copy-start(s32[1,4]{1,0:T(1,128)} %param.19) | copy-start | bytes 52
  97.9 5.1 %copy-start.4 = (bf16[64,8,512]{2,0,1:T(8,128)(2,1)}, bf16[64,8,512]{2,0,1:T(8,128)(2,1)S(1)}, u32[]{:S(2)}) copy-start(bf16[64,8,512]{2,0,1:T(8,128)(2,1)S(1)} %all-to-all-done.3) | copy-start | bytes 1572868
  97.9 17.9 %all-to-all-start.2 = ((bf16[64,8,512]{2,0,1:T(8,128)(2,1)}), bf16[64,8,512]{2,0,1:T(8,128)(2,1)}, u32[]{:S(2)}, u32[]{:S(2)}) async-start(bf16[64,8,512]{2,0,1:T(8,128)(2,1)} %copy.26), calls=%async_computation.2 | async-start | bytes 1048576 | tf_op jit(solution)/shard_map/all_to_all | solution.py:103
  102.1 172.7 %all-gather.7.cloned.1.call-start = ((), (), s32[]{:S(2)}) async-start(), calls=%async_computation.8 | async-start | bytes 10616832 | tf_op jit(solution)/shard_map/all_gather | solution.py:143
  166.8 6.0 %copy-start.6 = (bf16[8,512,64]{1,2,0:T(8,128)(2,1)S(1)}, bf16[8,512,64]{1,2,0:T(8,128)(2,1)}, u32[]{:S(2)}) copy-start(bf16[8,512,64]{1,2,0:T(8,128)(2,1)} %get-tuple-element.82) | copy-start | bytes 1572868
  168.3 31.7 %all-to-all-start.4 = ((bf16[8,64,512]{2,1,0:T(8,128)(2,1)}), bf16[8,64,512]{2,1,0:T(8,128)(2,1)S(1)}, u32[]{:S(2)}, u32[]{:S(2)}) async-start(bf16[8,64,512]{2,1,0:T(8,128)(2,1)} %copy.38), calls=%async_computation.4 | async-start | bytes 1048576 | tf_op jit(solution)/shard_map/all_to_all | solution.py:129
  173.3 33.0 %copy-start.7 = (bf16[8,512,64]{1,2,0:T(8,128)(2,1)S(1)}, bf16[8,512,64]{1,2,0:T(8,128)(2,1)}, u32[]{:S(2)}) copy-start(bf16[8,512,64]{1,2,0:T(8,128)(2,1)} %get-tuple-element.83) | copy-start | bytes 1572868
  200.1 32.9 %all-to-all-start.5 = ((bf16[8,64,512]{2,1,0:T(8,128)(2,1)}), bf16[8,64,512]{2,1,0:T(8,128)(2,1)S(1)}, u32[]{:S(2)}, u32[]{:S(2)}) async-start(bf16[8,64,512]{2,1,0:T(8,128)(2,1)} %copy.39), calls=%async_computation.5 | async-start | bytes 1048576 | tf_op jit(solution)/shard_map/all_to_all | solution.py:130
  206.8 32.8 %copy-start = (bf16[1,64,4,1536]{3,2,1,0:T(4,128)(2,1)S(1)}, bf16[1,64,4,1536]{3,2,1,0:T(4,128)(2,1)}, u32[]{:S(2)}) copy-start(bf16[1,64,4,1536]{3,2,1,0:T(4,128)(2,1)} %param.11) | copy-start | bytes 2359300
  232.9 33.0 %all-to-all-start.6 = ((bf16[8,64,512]{2,1,0:T(8,128)(2,1)}), bf16[8,64,512]{2,1,0:T(8,128)(2,1)}, u32[]{:S(2)}, u32[]{:S(2)}) async-start(bf16[8,64,512]{2,1,0:T(8,128)(2,1)} %copy.40), calls=%async_computation.6 | async-start | bytes 1048576 | tf_op jit(solution)/shard_map/all_to_all | solution.py:131
  239.7 1.4 copy-start.11
  242.7 32.1 %copy-start.10 = (bf16[256,1024]{1,0:T(8,128)(2,1)S(1)}, bf16[256,1024]{1,0:T(8,128)(2,1)}, u32[]{:S(2)}) copy-start(bf16[256,1024]{1,0:T(8,128)(2,1)} %reshape.137) | copy-start | bytes 1572868
  268.2 13.3 %copy-start.2 = (bf16[256,1536]{1,0:T(8,128)(2,1)S(1)}, bf16[256,1536]{1,0:T(8,128)(2,1)}, u32[]{:S(2)}) copy-start(bf16[256,1536]{1,0:T(8,128)(2,1)} %copy-done.1) | copy-start | bytes 2359300
  282.3 11.6 %collective-permute-start = (bf16[1,64,4,1536]{3,2,1,0:T(4,128)(2,1)S(1)}, bf16[1,64,4,1536]{3,2,1,0:T(4,128)(2,1)S(1)}, u32[]{:S(2)}, u32[]{:S(2)}) collective-permute-start(bf16[1,64,4,1536]{3,2,1,0:T(4,128)(2,1)S(1)} %reshape.140), channel_id=1, source_target_pairs={{0,24},{8,0},{16,8},{24,16},{1,25},{9,1},{17,9},{25,17},{2,26},{10... | collective-permute-start | bytes 2359304 | tf_op jit(solution)/shard_map/ppermute | solution.py:16
Sparse Core Ops, SparseCore 0:
  9.5 84.2 all-gather.4
  105.0 169.6 all-gather.6
where the time goes:
time: 303 us; the launch traced here: 302 us
  waiting for transfers between devices  147 us (49%)
  starting transfers between devices  56.3 us (19%)
  matrix products  51.9 us (17%)
  local copies, waits for them, and re-layouts  26.7 us (9%)
  between operations  13.7 us (5%)
  other arithmetic  5.78 us (2%)
    all_to_all x1, waiting for transfers between devices, on_device(): lax.all_to_all(join_items(query_grad), 'seq', split_axis=0, concat_axis=1...  25.2 us
    all_to_all x1, waiting for transfers between devices, on_device(): lax.all_to_all(join_items(key_gradient), 'seq', split_axis=0, concat_axis...  24.6 us
    all_to_all x1, waiting for transfers between devices, on_device(): lax.all_to_all(join_items(value_grad), 'seq', split_axis=0, concat_axis=1...  23.1 us
    all_gather x1, waiting for transfers between devices, project_grad(): lax.all_gather(out_rows, 'seq', axis=0, tiled=True)  18.9 us
    all_to_all x1, waiting for transfers between devices, on_device(): lax.all_to_all(frame_keys, 'seq', split_axis=1, concat_axis=0, tiled=True)  15.1 us
    dot_general x8, matrix products, step(): lax.dot_general(probs_low, grad_block, COL_DOT, preferred_element_type=jn...  14.8 us
    all_to_all x1, starting transfers between devices, on_device(): lax.all_to_all(frame_values, 'seq', split_axis=1, concat_axis=0, tiled=True)  14.4 us
    all_to_all x1, waiting for transfers between devices, on_device(): lax.all_to_all(frame_queries, 'seq', split_axis=1, concat_axis=0, tiled=T...  14 us
  transfers between devices with their start and end apart: 10, of which 9 were waited for; matrix products, arithmetic and copies ran while one was open for 25% of the time, Pallas kernels for 0%

commit v1 on v0

--- a/solution.py
+++ b/solution.py
@@ -9,6 +9,28 @@
 MASKED = -1e30
 ROW_DOT = (((1,), (1,)), ((), ()))
 COL_DOT = (((0,), (0,)), ((), ()))
+
+
+def joined_along(blocks, dim):
+    shape = list(blocks.shape[1:])
+    shape[dim] *= blocks.shape[0]
+    return jnp.moveaxis(blocks, 0, dim).reshape(shape)
+
+
+def gather_around(x, axis, dim):
+    length = lax.axis_size(axis)
+    pairs = [(i, (i + 1) % length) for i in range(length)]
+    back = [(b, a) for a, b in pairs]
+    lower, upper = ([], [])
+    for step in range(length - 1):
+        if step % 2 == 0:
+            lower.append(lax.ppermute(lower[-1] if lower else x, axis, pairs))
+        else:
+            upper.append(lax.ppermute(upper[-1] if upper else x, axis, back))
+    blocks = jnp.stack([*lower[::-1], x, *upper])
+    shift = lax.axis_index(axis) - len(lower)
+    blocks = blocks[(jnp.arange(length) - shift) % length]
+    return joined_along(blocks, dim)
 
 
 def shifted(shard, axis, by):
@@ -69,10 +91,7 @@
 
 def project_grad(flat_grad, out_rows):
     return lax.dot_general(
-        flat_grad,
-        lax.all_gather(out_rows, "seq", axis=0, tiled=True),
-        ROW_DOT,
-        preferred_element_type=jnp.float32,
+        flat_grad, gather_around(out_rows, "seq", 0), ROW_DOT, preferred_element_type=jnp.float32
     ).astype(jnp.bfloat16)
 
 

time: 303 us -> 325 us (1.073)
  local copies, waits for them, and re-layouts: 26.7 us -> 39.6 us
  starting transfers between devices: 56.3 us -> 64.4 us
    ppermute x0 -> x7, waiting for transfers between devices: none -> 29.2 us  [the longest x4 29.2 us: gather_around(): lower.append(lax.ppermute(lower[-1] if lower else x, axis, pairs))]
    ppermute x0 -> x7, starting transfers between devices: none -> 25.6 us  [the longest x3 19.1 us: gather_around(): upper.append(lax.ppermute(upper[-1] if upper else x, axis, back))]
    all_gather x1 -> x0, waiting for transfers between devices: 18.9 us -> none  [project_grad(): lax.all_gather(out_rows, 'seq', axis=0, tiled=True)]
    all_to_all x1, waiting for transfers between devices: 14 us -> 0.81 us  [on_device(): lax.all_to_all(frame_queries, 'seq', split_axis=1, concat_axis=0, tiled=T...]
    all_to_all x1, starting transfers between devices: 14.4 us -> 4.16 us  [on_device(): lax.all_to_all(frame_values, 'seq', split_axis=1, concat_axis=0, tiled=True)]
    unnamed x27 -> x36, local copies, waits for them, and re-layouts: 0.95 us -> 7.11 us
    all_to_all x1, waiting for transfers between devices: 0.01 us -> 4.41 us  [on_device(): lax.all_to_all(frame_values, 'seq', split_axis=1, concat_axis=0, tiled=True)]
    all_to_all x1, waiting for transfers between devices: 15.1 us -> 11.3 us  [on_device(): lax.all_to_all(frame_keys, 'seq', split_axis=1, concat_axis=0, tiled=True)]
  transfers between devices with their start and end apart: 10 -> 16, of which waited for: 9 -> 12; matrix products, arithmetic and copies ran while one was open for 25% -> 27% of each run, Pallas kernels for 0% -> 0%
where the time goes in v1:
time: 325 us; the launch traced here: 323 us
  waiting for transfers between devices  148 us (46%)
  starting transfers between devices  64.4 us (20%)
  matrix products  52.1 us (16%)
  local copies, waits for them, and re-layouts  39.6 us (12%)
  between operations  13.8 us (4%)
  other arithmetic  5.8 us (2%)
    ppermute x4, waiting for transfers between devices, gather_around(): lower.append(lax.ppermute(lower[-1] if lower else x, axis, pairs))  29.2 us
    all_to_all x1, waiting for transfers between devices, on_device(): lax.all_to_all(join_items(value_grad), 'seq', split_axis=0, concat_axis=1...  26.8 us
    all_to_all x1, waiting for transfers between devices, on_device(): lax.all_to_all(join_items(key_gradient), 'seq', split_axis=0, concat_axis...  26.3 us
    all_to_all x1, waiting for transfers between devices, on_device(): lax.all_to_all(join_items(query_grad), 'seq', split_axis=0, concat_axis=1...  24.7 us
    ppermute x3, starting transfers between devices, gather_around(): upper.append(lax.ppermute(upper[-1] if upper else x, axis, back))  19.1 us
    dot_general x8, matrix products, step(): lax.dot_general(probs_low, grad_block, COL_DOT, preferred_element_type=jn...  14.9 us
    all_to_all x1, starting transfers between devices, on_device(): lax.all_to_all(frame_keys, 'seq', split_axis=1, concat_axis=0, tiled=True)  13.2 us
    all_to_all x1, waiting for transfers between devices, on_device(): lax.all_to_all(frame_keys, 'seq', split_axis=1, concat_axis=0, tiled=True)  11.3 us
  transfers between devices with their start and end apart: 16, of which 12 were waited for; matrix products, arithmetic and copies ran while one was open for 27% of the time, Pallas kernels for 0%

profile of v1, /device:TPU:1, one launch (start us, length us, event | category | flops | bytes accessed | tf_op | source)
XLA Modules:
  0.0 323.4 jit_solution(13432602310754747131)
XLA Ops:
  6.5 2.1 collective-permute-start
  8.6 12.1 %collective-permute-done = bf16[128,1536]{1,0:T(8,128)(2,1)S(1)} collective-permute-done((bf16[128,1536]{1,0:T(8,128)(2,1)}, bf16[128,1536]{1,0:T(8,128)(2,1)S(1)}, u32[]{:S(2)}, u32[]{:S(2)}) %collective-permute-start) | collective-permute-done | bytes 393248 | tf_op jit(solution)/shard_map/ppermute | solution.py:27
  20.7 4.2 %collective-permute-start.4 = (bf16[128,1536]{1,0:T(8,128)(2,1)}, bf16[128,1536]{1,0:T(8,128)(2,1)S(1)}, u32[]{:S(2)}, u32[]{:S(2)}) collective-permute-start(bf16[128,1536]{1,0:T(8,128)(2,1)} %bitcast.125), channel_id=1, source_target_pairs={{1,0},{2,1},{3,2},{4,3},{5,4},{6,5},{7,6},{0,7},{9,8},{10,9},{11,1... | collective-permute-start | bytes 1179656 | tf_op jit(solution)/shard_map/ppermute | solution.py:29
  24.8 11.8 %collective-permute-done.1 = bf16[128,1536]{1,0:T(8,128)(2,1)S(1)} collective-permute-done((bf16[128,1536]{1,0:T(8,128)(2,1)S(1)}, bf16[128,1536]{1,0:T(8,128)(2,1)S(1)}, u32[]{:S(2)}, u32[]{:S(2)}) %collective-permute-start.1) | collective-permute-done | bytes 393248 | tf_op jit(solution)/shard_map/ppermute | solution.py:27
  36.6 2.2 collective-permute-start.2
  38.8 10.9 %collective-permute-start.5 = (bf16[128,1536]{1,0:T(8,128)(2,1)S(1)}, bf16[128,1536]{1,0:T(8,128)(2,1)}, u32[]{:S(2)}, u32[]{:S(2)}) collective-permute-start(bf16[128,1536]{1,0:T(8,128)(2,1)S(1)} %collective-permute-done.4), channel_id=1, source_target_pairs={{1,0},{2,1},{3,2},{4,3},{5,4},{6,5},{7,6},{0,7},{9,8},{10,9},{11,1... | collective-permute-start | bytes 1179656 | tf_op jit(solution)/shard_map/ppermute | solution.py:29
  49.7 5.4 %collective-permute-done.2 = bf16[128,1536]{1,0:T(8,128)(2,1)S(1)} collective-permute-done((bf16[128,1536]{1,0:T(8,128)(2,1)S(1)}, bf16[128,1536]{1,0:T(8,128)(2,1)S(1)}, u32[]{:S(2)}, u32[]{:S(2)}) %collective-permute-start.2) | collective-permute-done | bytes 393248 | tf_op jit(solution)/shard_map/ppermute | solution.py:27
  55.0 2.2 collective-permute-start.3
  59.4 4.2 %all-to-all-start = ((bf16[64,8,512]{2,0,1:T(8,128)(2,1)}), bf16[64,8,512]{2,0,1:T(8,128)(2,1)}, u32[]{:S(2)}, u32[]{:S(2)}) async-start(bf16[64,8,512]{2,0,1:T(8,128)(2,1)} %copy.40), calls=%async_computation | async-start | bytes 1048576 | tf_op jit(solution)/shard_map/all_to_all | solution.py:119
  66.8 4.1 %collective-permute-start.6 = (bf16[128,1536]{1,0:T(8,128)(2,1)}, bf16[128,1536]{1,0:T(8,128)(2,1)}, u32[]{:S(2)}, u32[]{:S(2)}) collective-permute-start(bf16[128,1536]{1,0:T(8,128)(2,1)} %collective-permute-done.5), channel_id=1, source_target_pairs={{1,0},{2,1},{3,2},{4,3},{5,4},{6,5},{7,6},{0,7},{9,8},{10,9},{11,1... | collective-permute-start | bytes 1179656 | tf_op jit(solution)/shard_map/ppermute | solution.py:29
  74.8 13.2 %all-to-all-start.1 = ((bf16[64,8,512]{2,0,1:T(8,128)(2,1)}), bf16[64,8,512]{2,0,1:T(8,128)(2,1)}, u32[]{:S(2)}, u32[]{:S(2)}) async-start(bf16[64,8,512]{2,0,1:T(8,128)(2,1)} %copy.41), calls=%async_computation.1 | async-start | bytes 1048576 | tf_op jit(solution)/shard_map/all_to_all | solution.py:120
  90.2 11.3 %all-to-all-done.1 = bf16[64,8,512]{2,0,1:T(8,128)(2,1)} async-done(((bf16[64,8,512]{2,0,1:T(8,128)(2,1)}), bf16[64,8,512]{2,0,1:T(8,128)(2,1)}, u32[]{:S(2)}, u32[]{:S(2)}) %all-to-all-start.1) | async-done | bytes 524320 | tf_op jit(solution)/shard_map/all_to_all | solution.py:120
  101.5 4.2 %all-to-all-start.3 = ((bf16[64,8,512]{2,0,1:T(8,128)(2,1)}), bf16[64,8,512]{2,0,1:T(8,128)(2,1)}, u32[]{:S(2)}, u32[]{:S(2)}) async-start(bf16[64,8,512]{2,0,1:T(8,128)(2,1)} %copy.44), calls=%async_computation.3 | async-start | bytes 1048576 | tf_op jit(solution)/shard_map/all_to_all | solution.py:121
  107.7 2.4 gather_fusion
  110.1 3.1 fusion.41
  114.5 4.4 %all-to-all-done.3 = bf16[64,8,512]{2,0,1:T(8,128)(2,1)} async-done(((bf16[64,8,512]{2,0,1:T(8,128)(2,1)}), bf16[64,8,512]{2,0,1:T(8,128)(2,1)}, u32[]{:S(2)}, u32[]{:S(2)}) %all-to-all-start.3) | async-done | bytes 524320 | tf_op jit(solution)/shard_map/all_to_all | solution.py:121
  118.9 4.2 %all-to-all-start.2 = ((bf16[64,8,512]{2,0,1:T(8,128)(2,1)}), bf16[64,8,512]{2,0,1:T(8,128)(2,1)}, u32[]{:S(2)}, u32[]{:S(2)}) async-start(bf16[64,8,512]{2,0,1:T(8,128)(2,1)} %copy.43), calls=%async_computation.2 | async-start | bytes 1048576 | tf_op jit(solution)/shard_map/all_to_all | solution.py:122
  130.5 6.0 %all-to-all-done.2 = bf16[64,8,512]{2,0,1:T(8,128)(2,1)} async-done(((bf16[64,8,512]{2,0,1:T(8,128)(2,1)}), bf16[64,8,512]{2,0,1:T(8,128)(2,1)}, u32[]{:S(2)}, u32[]{:S(2)}) %all-to-all-start.2) | async-done | bytes 524320 | tf_op jit(solution)/shard_map/all_to_all | solution.py:122
  139.3 46.5 %while.14 = (s32[]{:T(128)}, bf16[8,512,64]{1,2,0:T(8,128)(2,1)}, bf16[8,512,64]{1,2,0:T(8,128)(2,1)}, bf16[8,512,64]{1,2,0:T(8,128)(2,1)}, pred[8,512]{1,0:T(8,...) while((s32[]{:T(128)}, bf16[8,512,64]{1,2,0:T(8,128)(2,1)}, ...), condition=%wide.region_7.8_spmd, body=%wide.region_3.7_spmd.sunk | while | flops 172587520 | bytes 10056297 | solution.py:137
  139.9 1.9 fusion.72
  151.5 1.9 fusion.72
  157.3 1.9 fusion.72
  163.1 1.9 fusion.72
  189.1 4.3 %all-to-all-start.4 = ((bf16[8,64,512]{2,1,0:T(8,128)(2,1)}), bf16[8,64,512]{2,1,0:T(8,128)(2,1)S(1)}, u32[]{:S(2)}, u32[]{:S(2)}) async-start(bf16[8,64,512]{2,1,0:T(8,128)(2,1)} %copy.55), calls=%async_computation.4 | async-start | bytes 1048576 | tf_op jit(solution)/shard_map/all_to_all | solution.py:148
  195.4 24.7 %all-to-all-done.4 = bf16[8,64,512]{2,1,0:T(8,128)(2,1)S(1)} async-done(((bf16[8,64,512]{2,1,0:T(8,128)(2,1)}), bf16[8,64,512]{2,1,0:T(8,128)(2,1)S(1)}, u32[]{:S(2)}, u32[]{:S(2)}) %all-to-all-start.4) | async-done | bytes 524320 | tf_op jit(solution)/shard_map/all_to_all | solution.py:148
  220.2 3.7 %all-to-all-start.5 = ((bf16[8,64,512]{2,1,0:T(8,128)(2,1)}), bf16[8,64,512]{2,1,0:T(8,128)(2,1)S(1)}, u32[]{:S(2)}, u32[]{:S(2)}) async-start(bf16[8,64,512]{2,1,0:T(8,128)(2,1)} %copy.56), calls=%async_computation.5 | async-start | bytes 1048576 | tf_op jit(solution)/shard_map/all_to_all | solution.py:149
  227.0 26.3 %all-to-all-done.5 = bf16[8,64,512]{2,1,0:T(8,128)(2,1)S(1)} async-done(((bf16[8,64,512]{2,1,0:T(8,128)(2,1)}), bf16[8,64,512]{2,1,0:T(8,128)(2,1)S(1)}, u32[]{:S(2)}, u32[]{:S(2)}) %all-to-all-start.5) | async-done | bytes 524320 | tf_op jit(solution)/shard_map/all_to_all | solution.py:149
  253.3 4.2 %all-to-all-start.6 = ((bf16[8,64,512]{2,1,0:T(8,128)(2,1)}), bf16[8,64,512]{2,1,0:T(8,128)(2,1)}, u32[]{:S(2)}, u32[]{:S(2)}) async-start(bf16[8,64,512]{2,1,0:T(8,128)(2,1)} %copy.57), calls=%async_computation.6 | async-start | bytes 1048576 | tf_op jit(solution)/shard_map/all_to_all | solution.py:150
  260.7 26.8 %all-to-all-done.6 = bf16[8,64,512]{2,1,0:T(8,128)(2,1)} async-done(((bf16[8,64,512]{2,1,0:T(8,128)(2,1)}), bf16[8,64,512]{2,1,0:T(8,128)(2,1)}, u32[]{:S(2)}, u32[]{:S(2)}) %all-to-all-start.6) | async-done | bytes 524320 | tf_op jit(solution)/shard_map/all_to_all | solution.py:150
  289.7 6.8 %all-gather.3.cloned.1.call-done = bf16[1,1536,3072]{2,1,0:T(8,128)(2,1)} async-done(((bf16[1,192,3072]{2,1,0:T(8,128)(2,1)}), bf16[1,1536,3072]{2,1,0:T(8,128)(2,1)}) %all-gather.3.cloned.1.call-update) | async-done | bytes 9437200 | tf_op jit(solution)/shard_map/all_gather | solution.py:162
  296.5 6.7 %fusion.45 = (f32[256]{0:T(256)S(1)}, f32[256]{0:T(256)S(1)}, f32[256,1536]{1,0:T(8,128)S(1)}) fusion(f32[256]{0:T(256)S(1)} %sqrt.6, f32[256,1536]{1,0:T(8,128)S(1)} %reshape.194, f32[256]{0:T(256)S(1)} %div.47, f32[1536]{0:T(1024)S(1)} %reduce.3, bf16[1,1536,3072]{2,1,0:T(8,128)(2,1)} %all-gather.3.cloned.1.call-done, bf16[256,1024]{1,0:T(8,128)(2,1)} %reshape.192, ...), kind=kOutput, calls=%fused_computation.81 | convolution fusion | flops 2422996480 | bytes 14166016 | tf_op jit(solution)/shard_map/dot_general | solution.py:160
  305.0 10.8 %collective-permute-done.7 = bf16[1,64,4,1536]{3,2,1,0:T(4,128)(2,1)S(1)} collective-permute-done((bf16[1,64,4,1536]{3,2,1,0:T(4,128)(2,1)S(1)}, bf16[1,64,4,1536]{3,2,1,0:T(4,128)(2,1)S(1)}, u32[]{:S(2)}, u32[]{:S(2)}) %collective-permute-start.7) | collective-permute-done | bytes 786464 | tf_op jit(solution)/shard_map/ppermute | solution.py:38
  (155 shorter events, 80.3 us)
Async XLA Ops:
  6.5 57.0 %copy-start.2 = (bf16[1,64,4,1536]{3,2,1,0:T(4,128)(2,1)S(1)}, bf16[1,64,4,1536]{3,2,1,0:T(4,128)(2,1)}, u32[]{:S(2)}) copy-start(bf16[1,64,4,1536]{3,2,1,0:T(4,128)(2,1)} %param.16) | copy-start | bytes 2359300
  6.5 58.1 %copy-start.4 = (bf16[1,64,4,1024]{3,2,1,0:T(4,128)(2,1)S(1)}, bf16[1,64,4,1024]{3,2,1,0:T(4,128)(2,1)}, u32[]{:S(2)}) copy-start(bf16[1,64,4,1024]{3,2,1,0:T(4,128)(2,1)} %param.14) | copy-start | bytes 1572868
  6.5 14.1 %collective-permute-start = (bf16[128,1536]{1,0:T(8,128)(2,1)}, bf16[128,1536]{1,0:T(8,128)(2,1)S(1)}, u32[]{:S(2)}, u32[]{:S(2)}) collective-permute-start(bf16[128,1536]{1,0:T(8,128)(2,1)} %bitcast.124), channel_id=1, source_target_pairs={{0,1},{1,2},{2,3},{3,4},{4,5},{5,6},{6,7},{7,0},{8,9},{9,10},{10,1... | collective-permute-start | bytes 1179656 | tf_op jit(solution)/shard_map/ppermute | solution.py:27
  20.7 34.4 %copy-start.8 = (bf16[128,1536]{1,0:T(8,128)(2,1)}, bf16[128,1536]{1,0:T(8,128)(2,1)S(1)}, u32[]{:S(2)}) copy-start(bf16[128,1536]{1,0:T(8,128)(2,1)S(1)} %collective-permute-done) | copy-start | bytes 1179652
  20.7 15.9 %collective-permute-start.1 = (bf16[128,1536]{1,0:T(8,128)(2,1)S(1)}, bf16[128,1536]{1,0:T(8,128)(2,1)S(1)}, u32[]{:S(2)}, u32[]{:S(2)}) collective-permute-start(bf16[128,1536]{1,0:T(8,128)(2,1)S(1)} %collective-permute-done), channel_id=1, source_target_pairs={{0,1},{1,2},{2,3},{3,4},{4,5},{5,6},{6,7},{7,0},{8,9},{9,10},{10,1... | collective-permute-start | bytes 1179656 | tf_op jit(solution)/shard_map/ppermute | solution.py:27
  20.7 18.1 %collective-permute-start.4 = (bf16[128,1536]{1,0:T(8,128)(2,1)}, bf16[128,1536]{1,0:T(8,128)(2,1)S(1)}, u32[]{:S(2)}, u32[]{:S(2)}) collective-permute-start(bf16[128,1536]{1,0:T(8,128)(2,1)} %bitcast.125), channel_id=1, source_target_pairs={{1,0},{2,1},{3,2},{4,3},{5,4},{6,5},{7,6},{0,7},{9,8},{10,9},{11,1... | collective-permute-start | bytes 1179656 | tf_op jit(solution)/shard_map/ppermute | solution.py:29
  36.6 20.6 %copy-start.10 = (bf16[128,1536]{1,0:T(8,128)(2,1)}, bf16[128,1536]{1,0:T(8,128)(2,1)S(1)}, u32[]{:S(2)}) copy-start(bf16[128,1536]{1,0:T(8,128)(2,1)S(1)} %collective-permute-done.1) | copy-start | bytes 1179652
  36.6 18.4 %collective-permute-start.2 = (bf16[128,1536]{1,0:T(8,128)(2,1)S(1)}, bf16[128,1536]{1,0:T(8,128)(2,1)S(1)}, u32[]{:S(2)}, u32[]{:S(2)}) collective-permute-start(bf16[128,1536]{1,0:T(8,128)(2,1)S(1)} %collective-permute-done.1), channel_id=1, source_target_pairs={{0,1},{1,2},{2,3},{3,4},{4,5},{5,6},{6,7},{7,0},{8,9},{9,10},{10,1... | collective-permute-start | bytes 1179656 | tf_op jit(solution)/shard_map/ppermute | solution.py:27
  38.8 26.9 %copy-start.9 = (bf16[128,1536]{1,0:T(8,128)(2,1)}, bf16[128,1536]{1,0:T(8,128)(2,1)S(1)}, u32[]{:S(2)}) copy-start(bf16[128,1536]{1,0:T(8,128)(2,1)S(1)} %collective-permute-done.4) | copy-start | bytes 1179652
  38.8 28.0 %collective-permute-start.5 = (bf16[128,1536]{1,0:T(8,128)(2,1)S(1)}, bf16[128,1536]{1,0:T(8,128)(2,1)}, u32[]{:S(2)}, u32[]{:S(2)}) collective-permute-start(bf16[128,1536]{1,0:T(8,128)(2,1)S(1)} %collective-permute-done.4), channel_id=1, source_target_pairs={{1,0},{2,1},{3,2},{4,3},{5,4},{6,5},{7,6},{0,7},{9,8},{10,9},{11,1... | collective-permute-start | bytes 1179656 | tf_op jit(solution)/shard_map/ppermute | solution.py:29
  55.0 10.7 %copy-start.11 = (bf16[128,1536]{1,0:T(8,128)(2,1)}, bf16[128,1536]{1,0:T(8,128)(2,1)S(1)}, u32[]{:S(2)}) copy-start(bf16[128,1536]{1,0:T(8,128)(2,1)S(1)} %collective-permute-done.2) | copy-start | bytes 1179652
  55.0 15.9 %collective-permute-start.3 = (bf16[128,1536]{1,0:T(8,128)(2,1)S(1)}, bf16[128,1536]{1,0:T(8,128)(2,1)}, u32[]{:S(2)}, u32[]{:S(2)}) collective-permute-start(bf16[128,1536]{1,0:T(8,128)(2,1)S(1)} %collective-permute-done.2), channel_id=1, source_target_pairs={{0,1},{1,2},{2,3},{3,4},{4,5},{5,6},{6,7},{7,0},{8,9},{9,10},{10,1... | collective-permute-start | bytes 1179656 | tf_op jit(solution)/shard_map/ppermute | solution.py:27
  58.4 7.3 %copy-start.5 = (bf16[1,64,4,1024]{3,2,1,0:T(4,128)(2,1)S(1)}, bf16[1,64,4,1024]{3,2,1,0:T(4,128)(2,1)}, u32[]{:S(2)}) copy-start(bf16[1,64,4,1024]{3,2,1,0:T(4,128)(2,1)} %param.15) | copy-start | bytes 1572868
  59.4 15.5 %all-to-all-start = ((bf16[64,8,512]{2,0,1:T(8,128)(2,1)}), bf16[64,8,512]{2,0,1:T(8,128)(2,1)}, u32[]{:S(2)}, u32[]{:S(2)}) async-start(bf16[64,8,512]{2,0,1:T(8,128)(2,1)} %copy.40), calls=%async_computation | async-start | bytes 1048576 | tf_op jit(solution)/shard_map/all_to_all | solution.py:119
  65.7 23.4 %copy-start.7 = (bf16[1,128,1536]{2,1,0:T(8,128)(2,1)S(1)}, bf16[1,128,1536]{2,1,0:T(8,128)(2,1)}, u32[]{:S(2)}) copy-start(bf16[1,128,1536]{2,1,0:T(8,128)(2,1)} %param.17) | copy-start | bytes 1179652
  66.8 39.8 %collective-permute-start.6 = (bf16[128,1536]{1,0:T(8,128)(2,1)}, bf16[128,1536]{1,0:T(8,128)(2,1)}, u32[]{:S(2)}, u32[]{:S(2)}) collective-permute-start(bf16[128,1536]{1,0:T(8,128)(2,1)} %collective-permute-done.5), channel_id=1, source_target_pairs={{1,0},{2,1},{3,2},{4,3},{5,4},{6,5},{7,6},{0,7},{9,8},{10,9},{11,1... | collective-permute-start | bytes 1179656 | tf_op jit(solution)/shard_map/ppermute | solution.py:29
  74.8 26.6 %all-to-all-start.1 = ((bf16[64,8,512]{2,0,1:T(8,128)(2,1)}), bf16[64,8,512]{2,0,1:T(8,128)(2,1)}, u32[]{:S(2)}, u32[]{:S(2)}) async-start(bf16[64,8,512]{2,0,1:T(8,128)(2,1)} %copy.41), calls=%async_computation.1 | async-start | bytes 1048576 | tf_op jit(solution)/shard_map/all_to_all | solution.py:120
  101.5 17.5 %all-to-all-start.3 = ((bf16[64,8,512]{2,0,1:T(8,128)(2,1)}), bf16[64,8,512]{2,0,1:T(8,128)(2,1)}, u32[]{:S(2)}, u32[]{:S(2)}) async-start(bf16[64,8,512]{2,0,1:T(8,128)(2,1)} %copy.44), calls=%async_computation.3 | async-start | bytes 1048576 | tf_op jit(solution)/shard_map/all_to_all | solution.py:121
  113.2 10.7 %copy-start.13 = (s32[1,4]{1,0:T(1,128)S(1)}, s32[1,4]{1,0:T(1,128)}, u32[]{:S(2)}) copy-start(s32[1,4]{1,0:T(1,128)} %param.19) | copy-start | bytes 52
  118.9 17.5 %all-to-all-start.2 = ((bf16[64,8,512]{2,0,1:T(8,128)(2,1)}), bf16[64,8,512]{2,0,1:T(8,128)(2,1)}, u32[]{:S(2)}, u32[]{:S(2)}) async-start(bf16[64,8,512]{2,0,1:T(8,128)(2,1)} %copy.43), calls=%async_computation.2 | async-start | bytes 1048576 | tf_op jit(solution)/shard_map/all_to_all | solution.py:122
  123.1 173.3 %all-gather.3.cloned.1.call-start = ((), (), s32[]{:S(2)}) async-start(), calls=%async_computation.7 | async-start | bytes 10616832 | tf_op jit(solution)/shard_map/all_gather | solution.py:162
  185.8 7.5 %copy-start.3 = (bf16[8,512,64]{1,2,0:T(8,128)(2,1)S(1)}, bf16[8,512,64]{1,2,0:T(8,128)(2,1)}, u32[]{:S(2)}) copy-start(bf16[8,512,64]{1,2,0:T(8,128)(2,1)} %get-tuple-element.82) | copy-start | bytes 1572868
  189.1 31.1 %all-to-all-start.4 = ((bf16[8,64,512]{2,1,0:T(8,128)(2,1)}), bf16[8,64,512]{2,1,0:T(8,128)(2,1)S(1)}, u32[]{:S(2)}, u32[]{:S(2)}) async-start(bf16[8,64,512]{2,1,0:T(8,128)(2,1)} %copy.55), calls=%async_computation.4 | async-start | bytes 1048576 | tf_op jit(solution)/shard_map/all_to_all | solution.py:148
  193.9 63.6 %copy-start = (bf16[1,64,4,1536]{3,2,1,0:T(4,128)(2,1)S(1)}, bf16[1,64,4,1536]{3,2,1,0:T(4,128)(2,1)}, u32[]{:S(2)}) copy-start(bf16[1,64,4,1536]{3,2,1,0:T(4,128)(2,1)} %param.11) | copy-start | bytes 2359300
  220.2 33.2 %all-to-all-start.5 = ((bf16[8,64,512]{2,1,0:T(8,128)(2,1)}), bf16[8,64,512]{2,1,0:T(8,128)(2,1)S(1)}, u32[]{:S(2)}, u32[]{:S(2)}) async-start(bf16[8,64,512]{2,1,0:T(8,128)(2,1)} %copy.56), calls=%async_computation.5 | async-start | bytes 1048576 | tf_op jit(solution)/shard_map/all_to_all | solution.py:149
  225.5 33.4 %copy-start.12 = (f32[1,1536]{1,0:T(1,128)S(1)}, f32[1,1536]{1,0:T(1,128)}, u32[]{:S(2)}) copy-start(f32[1,1536]{1,0:T(1,128)} %param.12) | copy-start | bytes 18436
  253.3 34.1 %all-to-all-start.6 = ((bf16[8,64,512]{2,1,0:T(8,128)(2,1)}), bf16[8,64,512]{2,1,0:T(8,128)(2,1)}, u32[]{:S(2)}, u32[]{:S(2)}) async-start(bf16[8,64,512]{2,1,0:T(8,128)(2,1)} %copy.57), calls=%async_computation.6 | async-start | bytes 1048576 | tf_op jit(solution)/shard_map/all_to_all | solution.py:150
  260.2 36.3 %copy-start.6 = (bf16[256,1024]{1,0:T(8,128)(2,1)S(1)}, bf16[256,1024]{1,0:T(8,128)(2,1)}, u32[]{:S(2)}) copy-start(bf16[256,1024]{1,0:T(8,128)(2,1)} %reshape.190) | copy-start | bytes 1572868
  289.7 13.5 %copy-start.1 = (bf16[256,1536]{1,0:T(8,128)(2,1)S(1)}, bf16[256,1536]{1,0:T(8,128)(2,1)}, u32[]{:S(2)}) copy-start(bf16[256,1536]{1,0:T(8,128)(2,1)} %reshape_squeeze.2) | copy-start | bytes 2359300
  304.1 11.7 %collective-permute-start.7 = (bf16[1,64,4,1536]{3,2,1,0:T(4,128)(2,1)S(1)}, bf16[1,64,4,1536]{3,2,1,0:T(4,128)(2,1)S(1)}, u32[]{:S(2)}, u32[]{:S(2)}) collective-permute-start(bf16[1,64,4,1536]{3,2,1,0:T(4,128)(2,1)S(1)} %reshape.193), channel_id=1, source_target_pairs={{0,24},{8,0},{16,8},{24,16},{1,25},{9,1},{17,9},{25,17},{2,26},{10... | collective-permute-start | bytes 2359304 | tf_op jit(solution)/shard_map/ppermute | solution.py:38
Sparse Core Ops, SparseCore 0:
  126.1 170.3 all-gather.2
